TPU v7x, 512 devices: a whole 4x8x8 slice. The times are simulated.
512 devices in a mesh: row: 32 (over z, x), col: 16 (over y, core).
Axes of the slice: x: 4, y: 8, z: 8, core: 2. Of those that a mesh axis runs over, the one named last changes fastest.
Arguments:
- panel: float32 [9216, 256], P(('row', 'col')), may hold values from -60 to 636, as said below
- trailing: float32 [9216, 9216], P('row', 'col'), may hold values from -9 to 9
Outputs:
- updated: float32 [9216, 9216], P('row', 'col')
Inputs may be any that keep to these rules, and one draw needn't show every extreme that they name: The panel's first 256 rows carry a positive diagonal between 288 and 576 on top of the other entries.
All inputs are finite; a program needn't handle non-finite values.
Results may differ from a plain program's by a relative error of at most 0.00017.
Values sent between devices are 32-bit elements; how exact they have to be, the bound alone decides.
No kernel may reach another device: no remote copies, remote signals or barrier semaphores. Data moves between devices by JAX's collectives and lax.ppermute only.
A program may use at most 64 MiB of HBM per device.

v0:
```python
import jax
import jax.numpy as jnp
from jax import lax
from jax.sharding import PartitionSpec as P


def spread(shard, axis, root):
    mine = lax.axis_index(axis) == root
    return lax.psum(jnp.where(mine, shard, jnp.zeros_like(shard)), axis)


def matmul(left, right):
    return jnp.dot(left, right, precision=lax.Precision.HIGHEST, preferred_element_type=jnp.float32)


def inner_rows(left, right):
    return lax.dot_general(
        left,
        right,
        (((0,), (0,)), ((), ())),
        precision=lax.Precision.HIGHEST,
        preferred_element_type=jnp.float32,
    )


def on_device(panel, trailing):
    n_col = lax.axis_size("col")
    n_row = lax.axis_size("row")
    fold = n_row // n_col
    local_rows = panel.shape[0]
    width = panel.shape[1]
    first_row = (lax.axis_index("row") * n_col + lax.axis_index("col")) * local_rows
    global_rows = first_row + jnp.arange(local_rows, dtype=jnp.int32)
    picker = (jnp.arange(width, dtype=jnp.int32)[:, None] == global_rows[None, :]).astype(
        jnp.float32
    )
    ident = jnp.eye(width, dtype=jnp.float32)
    gram_part = inner_rows(panel, panel)
    top_part = matmul(picker, panel)
    gram, top = lax.psum((gram_part, top_part), ("row", "col"))
    lower = jnp.linalg.cholesky(gram)
    basis = jax.scipy.linalg.solve_triangular(lower, panel.T, lower=True).T
    corner = jax.scipy.linalg.solve_triangular(lower, top.T, lower=True).T
    w_local = basis + picker.T
    w_rows = lax.all_gather(w_local, "col", axis=0, tiled=True)
    square = ident + corner
    normal_eq = inner_rows(square, square)
    tmat = jax.scipy.linalg.cho_solve((jnp.linalg.cholesky(normal_eq), True), square.T)
    col_owner = lax.axis_index("col") * fold
    w_cols = jnp.concatenate([spread(w_rows, "row", col_owner + step) for step in range(fold)], 0)
    y_local = lax.psum_scatter(matmul(trailing, w_cols), "col", scatter_dimension=0, tiled=True)
    x_local = matmul(y_local, tmat)
    inner = lax.psum(inner_rows(w_local, x_local), ("row", "col"))
    small = matmul(tmat.T, inner)
    z_local = x_local - 0.5 * matmul(w_local, small)
    z_rows = lax.all_gather(z_local, "col", axis=0, tiled=True)
    z_cols = jnp.concatenate([spread(z_rows, "row", col_owner + step) for step in range(fold)], 0)
    left = jnp.concatenate([z_rows, w_rows], 1)
    right = jnp.concatenate([w_cols, z_cols], 1)
    update = lax.dot_general(
        left,
        right,
        (((1,), (1,)), ((), ())),
        precision=lax.Precision.HIGHEST,
        preferred_element_type=jnp.float32,
    )
    return trailing - update


def solution(mesh):
    return jax.shard_map(
        on_device,
        mesh=mesh,
        in_specs=(P(("row", "col"), None), P("row", "col")),
        out_specs=P("row", "col"),
        check_vma=False,
    )
```

profile of v0, /device:TPU:8, one launch (start us, length us, event | category | flops | bytes accessed | tf_op | source)
XLA Modules:
  0.0 1168.6 jit_solution(10823113499661705974)
XLA Ops:
  6.5 1.9 fusion.51
  8.5 1.7 convolution_bitcast_fusion.1
  10.2 1.3 dynamic-slice.11
  12.2 277.5 %all-reduce.15.cloned.1.call-done = (f32[256,256]{0,1:T(8,128)}, f32[256,256]{0,1:T(8,128)}) async-done(((f32[256,256]{0,1:T(8,128)}, f32[256,256]{0,1:T(8,128)}), (f32[256,256]{0,1:T(8,128)}, f32[256,256]{0,1:T(8,128)})) %all-reduce.15.cloned.1.call-update) | async-done | bytes 524304 | tf_op jit(solution)/shard_map/psum | solution.py:40
  289.7 1.1 copy.10
  290.7 1.0 fusion.12
  291.7 11.7 %cholesky.130 = f32[128,128]{1,0:T(8,128)S(1)} custom-call(f32[128,128]{1,0:T(8,128)S(1)} %cholesky.194), custom_call_target="Cholesky" | custom-call | tf_op jit(solution)/shard_map/jit(cholesky)/cholesky | solution.py:41
  303.5 9.8 custom-call.23
  313.3 0.2 constant_dynamic-update-slice_fusion.5
  313.5 0.3 convolution_subtract_fusion.5
  313.8 11.7 %cholesky.147 = f32[128,128]{1,0:T(8,128)S(1)} custom-call(f32[128,128]{1,0:T(8,128)S(1)} %convolution_subtract_fusion.5), custom_call_target="Cholesky" | custom-call | tf_op jit(solution)/shard_map/jit(cholesky)/cholesky | solution.py:41
  325.6 0.7 compare_reduce_fusion.2
  327.6 0.1 triangular_solve.104
  327.7 4.0 while.6
  327.7 0.6 fusion.75
  328.3 1.4 bitcast_dynamic-update-slice_fusion.4
  329.7 0.6 fusion.75
  330.3 1.4 bitcast_dynamic-update-slice_fusion.4
  331.6 19.9 %custom-call.19 = f32[2,128,128]{1,2,0:T(8,128)S(1)} custom-call(f32[2,128,128]{2,1,0:T(8,128)S(1)} %get-tuple-element.22), custom_call_target="InvertDiagBlocksLowerTriangular" | custom-call | tf_op jit(solution)/shard_map/jit(_solve_triangular)/triangular_solve | solution.py:42
  351.5 0.3 fusion.18
  351.8 0.4 convolution_subtract_fusion.3
  352.2 0.3 fusion.29
  352.6 0.4 fusion.11
  353.0 0.2 fusion.28
  353.2 0.2 convolution_subtract_fusion.6
  353.4 0.2 fusion.30
  353.6 0.1 fusion.48
  353.7 0.1 copy.13
  353.9 11.7 %cholesky.164 = f32[128,128]{1,0:T(8,128)S(1)} custom-call(f32[128,128]{1,0:T(8,128)S(1)} %cholesky.197), custom_call_target="Cholesky" | custom-call | tf_op jit(solution)/shard_map/jit(cholesky)/cholesky | solution.py:48
  365.6 0.6 compare_reduce_fusion.1
  366.3 9.8 custom-call.25
  376.1 0.2 constant_dynamic-update-slice_fusion.2
  376.3 0.3 convolution_subtract_fusion.4
  376.6 11.7 %cholesky.181 = f32[128,128]{1,0:T(8,128)S(1)} custom-call(f32[128,128]{1,0:T(8,128)S(1)} %convolution_subtract_fusion.4), custom_call_target="Cholesky" | custom-call | tf_op jit(solution)/shard_map/jit(cholesky)/cholesky | solution.py:48
  388.3 0.7 compare_reduce_fusion
  390.5 4.1 while.7
  390.5 0.6 fusion.76
  391.1 1.4 bitcast_dynamic-update-slice_fusion.5
  392.5 0.6 fusion.76
  393.1 1.4 bitcast_dynamic-update-slice_fusion.5
  394.6 19.9 %custom-call.20 = f32[2,128,128]{1,2,0:T(8,128)S(1)} custom-call(f32[2,128,128]{2,1,0:T(8,128)S(1)} %get-tuple-element.30), custom_call_target="InvertDiagBlocksLowerTriangular" | custom-call | tf_op jit(solution)/shard_map/jit(_cho_solve)/triangular_solve | solution.py:48
  414.5 0.3 fusion.16
  414.8 0.3 convolution_subtract_fusion.2
  415.1 16.0 %all-gather = f32[16,18,256]{2,1,0:T(8,128)S(1)} all-gather(f32[1,18,256]{2,1,0:T(8,128)S(1)} %fusion.48), channel_id=1, replica_groups=mesh['row'=32,'col'=16] {'col'}, dimensions={0}, use_global_device_ids=true | all-gather | bytes 313344 | tf_op jit(solution)/shard_map/all_gather | solution.py:45
  431.2 0.8 broadcast_select_fusion.2
  432.1 0.3 fusion.32
  432.4 0.3 fusion.33
  432.7 0.3 convolution_subtract_fusion.1
  433.0 156.9 %all-reduce.19.cloned.1.call-done = (f32[288,256]{1,0:T(8,128)}, f32[288,256]{1,0:T(8,128)}) async-done(((f32[288,256]{1,0:T(8,128)}, f32[288,256]{1,0:T(8,128)}), (f32[288,256]{1,0:T(8,128)}, f32[288,256]{1,0:T(8,128)})) %all-reduce.19.cloned.1.call-update) | async-done | bytes 589840 | tf_op jit(solution)/shard_map/psum | solution.py:9
  589.9 1.0 constant_dynamic-update-slice_fusion.1
  591.0 0.9 convolution_bitcast_fusion
  591.9 0.9 copy.11
  592.8 0.0 all-reduce.11.cloned.1.call-start
  592.9 0.3 fusion.31
  593.2 111.0 %all-reduce.13.cloned.1.call-done = f32[288,256]{0,1:T(8,128)} async-done(((f32[288,256]{0,1:T(8,128)}), f32[288,256]{0,1:T(8,128)}) %all-reduce.13.cloned.1.call-update) | async-done | bytes 294928
  704.2 1.3 fusion.15
  705.5 1.2 fusion.46
  706.8 275.7 %all-reduce.11.cloned.1.call-done = f32[256,256]{1,0:T(8,128)} async-done(((f32[256,256]{1,0:T(8,128)}), f32[256,256]{1,0:T(8,128)}) %all-reduce.11.cloned.1.call-update) | async-done | bytes 262160 | tf_op jit(solution)/shard_map/psum | solution.py:53
  982.5 1.5 fusion.14
  984.0 0.3 fusion.6
  984.3 15.7 %all-gather.1 = f32[16,18,256]{2,1,0:T(8,128)S(1)} all-gather(f32[1,18,256]{2,1,0:T(8,128)S(1)} %fusion.6), channel_id=1, replica_groups=mesh['row'=32,'col'=16] {'col'}, dimensions={0}, use_global_device_ids=true | all-gather | bytes 313344 | tf_op jit(solution)/shard_map/all_gather | solution.py:56
  1000.1 0.8 broadcast_select_fusion.1
  1000.9 157.6 %all-reduce.17.cloned.1.call-done = (f32[288,256]{1,0:T(8,128)}, f32[288,256]{1,0:T(8,128)}) async-done(((f32[288,256]{1,0:T(8,128)}, f32[288,256]{1,0:T(8,128)}), (f32[288,256]{1,0:T(8,128)}, f32[288,256]{1,0:T(8,128)})) %all-reduce.17.cloned.1.call-update) | async-done | bytes 589840 | tf_op jit(solution)/shard_map/psum | solution.py:9
  1158.5 3.5 convolution_subtract_fusion
  (40 shorter events, 0.7 us)
Async XLA Ops:
  6.5 283.1 %all-reduce.15.cloned.1.call-start = ((), (), s32[]{:S(2)}) async-start(), calls=%async_computation.2 | async-start | bytes 1048576 | tf_op jit(solution)/shard_map/psum | solution.py:40
  10.2 579.7 %all-reduce.19.cloned.1.call-start = ((), (), s32[]{:S(2)}) async-start(), calls=%async_computation.4 | async-start | bytes 1179648 | tf_op jit(solution)/shard_map/psum | solution.py:9
  327.5 24.0 %copy-start.3 = (f32[256,256]{0,1:T(8,128)S(1)}, f32[256,256]{0,1:T(8,128)}, u32[]{:S(2)}) copy-start(f32[256,256]{0,1:T(8,128)} %get-tuple-element.55) | copy-start | bytes 786436
  352.2 0.8 copy-start.1
  432.0 272.1 %all-reduce.13.cloned.1.call-start = ((), (), s32[]{:S(2)}) async-start(), calls=%async_computation.1 | async-start | bytes 786432
  432.7 158.3 %copy-start = (f32[288,576]{1,0:T(8,128)S(1)}, f32[288,576]{1,0:T(8,128)}, u32[]{:S(2)}) copy-start(f32[288,576]{1,0:T(8,128)} %param.6) | copy-start | bytes 1990660
  589.9 1.1 copy-start.2
  592.8 389.6 %all-reduce.11.cloned.1.call-start = ((), (), s32[]{:S(2)}) async-start(), calls=%async_computation | async-start | bytes 524288 | tf_op jit(solution)/shard_map/psum | solution.py:53
  706.8 451.8 %all-reduce.17.cloned.1.call-start = ((), (), s32[]{:S(2)}) async-start(), calls=%async_computation.3 | async-start | bytes 1179648 | tf_op jit(solution)/shard_map/psum | solution.py:9
Sparse Core Ops, SparseCore 0:
  12.5 277.0 all-reduce.14
  432.1 157.7 all-reduce.18
  593.0 111.1 all-reduce.12
  709.0 273.4 all-reduce.10
  1001.1 157.4 all-reduce.16
where the time goes:
time: 1170 us
  waiting for transfers between devices  979 us (84%)
  other arithmetic  111 us (9%)
  blocking collectives  31.8 us (3%)
  matrix products  17.1 us (1%)
  between operations  16.8 us (1%)
  local copies, waits for them, and re-layouts  12.7 us (1%)
    psum x2, waiting for transfers between devices, spread(): return lax.psum(jnp.where(mine, shard, jnp.zeros_like(shard)), axis)  315 us
    psum x1, waiting for transfers between devices, on_device(): gram, top = lax.psum((gram_part, top_part), ('row', 'col'))  277 us
    psum x1, waiting for transfers between devices, on_device(): inner = lax.psum(inner_rows(w_local, x_local), ('row', 'col'))  276 us
    unnamed x6, waiting for transfers between devices  111 us
    another operation x7, other arithmetic, on_device(): jnp.linalg.cholesky(normal_eq)  34.7 us
    another operation x6, other arithmetic, on_device(): lower = jnp.linalg.cholesky(gram)  34 us
  transfers between devices with their start and end apart: 5, of which 5 were waited for; matrix products, arithmetic and copies ran while one was open for 0% of the time, Pallas kernels for 0%

commit v1 on v0

--- a/solution.py
+++ b/solution.py
@@ -37,7 +37,7 @@
     ident = jnp.eye(width, dtype=jnp.float32)
     gram_part = inner_rows(panel, panel)
     top_part = matmul(picker, panel)
-    gram, top = lax.psum((gram_part, top_part), ("row", "col"))
+    gram, top = lax.psum(lax.psum((gram_part, top_part), "col"), "row")
     lower = jnp.linalg.cholesky(gram)
     basis = jax.scipy.linalg.solve_triangular(lower, panel.T, lower=True).T
     corner = jax.scipy.linalg.solve_triangular(lower, top.T, lower=True).T

time: 1170 us -> 1110 us (0.949)
  waiting for transfers between devices: 979 us -> 919 us
    psum x1 -> x3, waiting for transfers between devices: 277 us -> 436 us  [on_device(): gram, top = lax.psum(lax.psum((gram_part, top_part), 'col'), 'row')]
    psum x2 -> x1, waiting for transfers between devices: 315 us -> 158 us  [spread(): return lax.psum(jnp.where(mine, shard, jnp.zeros_like(shard)), axis)]
    unnamed x6 -> x7, waiting for transfers between devices: 111 us -> 49.3 us
  transfers between devices with their start and end apart: 5 -> 6, of which waited for: 5 -> 6; matrix products, arithmetic and copies ran while one was open for 0% -> 6% of each run, Pallas kernels for 0% -> 0%
where the time goes in v1:
time: 1110 us
  waiting for transfers between devices  919 us (83%)
  other arithmetic  111 us (10%)
  blocking collectives  32.5 us (3%)
  matrix products  18.9 us (2%)
  between operations  17 us (2%)
  local copies, waits for them, and re-layouts  12.8 us (1%)
    psum x3, waiting for transfers between devices, on_device(): gram, top = lax.psum(lax.psum((gram_part, top_part), 'col'), 'row')  436 us
    psum x1, waiting for transfers between devices, on_device(): inner = lax.psum(inner_rows(w_local, x_local), ('row', 'col'))  276 us
    psum x1, waiting for transfers between devices, spread(): return lax.psum(jnp.where(mine, shard, jnp.zeros_like(shard)), axis)  158 us
    unnamed x7, waiting for transfers between devices  49.3 us
    another operation x7, other arithmetic, on_device(): jnp.linalg.cholesky(normal_eq)  34.7 us
    another operation x6, other arithmetic, on_device(): lower = jnp.linalg.cholesky(gram)  34 us
  transfers between devices with their start and end apart: 6, of which 6 were waited for; matrix products, arithmetic and copies ran while one was open for 6% of the time, Pallas kernels for 0%

profile of v1, /device:TPU:8, one launch (start us, length us, event | category | flops | bytes accessed | tf_op | source)
XLA Modules:
  0.0 1111.6 jit_solution(368729887928413516)
XLA Ops:
  6.5 1.9 fusion.52
  8.5 1.7 fusion.21
  10.2 119.2 %all-reduce.22.cloned.1.call-done = (f32[256,256]{1,0:T(8,128)}, f32[256,256]{0,1:T(8,128)}) async-done(((f32[256,256]{1,0:T(8,128)}, f32[256,256]{0,1:T(8,128)}), (f32[256,256]{1,0:T(8,128)}, f32[256,256]{0,1:T(8,128)})) %all-reduce.22.cloned.1.call-update) | async-done | bytes 524304 | tf_op jit(solution)/shard_map/psum | solution.py:40
  129.6 162.8 %all-reduce.12.cloned.1.call-done = f32[256,256]{0,1:T(8,128)} async-done(((f32[256,256]{0,1:T(8,128)}), f32[256,256]{0,1:T(8,128)}) %all-reduce.12.cloned.1.call-update) | async-done | bytes 262160 | tf_op jit(solution)/shard_map/psum | solution.py:40
  292.4 1.1 copy.10
  293.5 1.0 fusion.12
  294.5 11.7 %cholesky.130 = f32[128,128]{1,0:T(8,128)S(1)} custom-call(f32[128,128]{1,0:T(8,128)S(1)} %cholesky.194), custom_call_target="Cholesky" | custom-call | tf_op jit(solution)/shard_map/jit(cholesky)/cholesky | solution.py:41
  306.2 9.8 custom-call.23
  316.1 0.2 constant_dynamic-update-slice_fusion.5
  316.3 0.3 convolution_subtract_fusion.5
  316.6 11.7 %cholesky.147 = f32[128,128]{1,0:T(8,128)S(1)} custom-call(f32[128,128]{1,0:T(8,128)S(1)} %convolution_subtract_fusion.5), custom_call_target="Cholesky" | custom-call | tf_op jit(solution)/shard_map/jit(cholesky)/cholesky | solution.py:41
  328.3 0.7 compare_reduce_fusion.2
  330.4 4.2 while.6
  330.6 0.6 fusion.76
  331.3 1.3 bitcast_dynamic-update-slice_fusion.4
  332.6 0.6 fusion.76
  333.3 1.3 bitcast_dynamic-update-slice_fusion.4
  334.7 19.7 %custom-call.19 = f32[2,128,128]{1,2,0:T(8,128)S(1)} custom-call(f32[2,128,128]{2,1,0:T(8,128)S(1)} %get-tuple-element.22), custom_call_target="InvertDiagBlocksLowerTriangular" | custom-call | tf_op jit(solution)/shard_map/jit(_solve_triangular)/triangular_solve | solution.py:42
  354.3 0.2 fusion.29
  354.5 0.2 convolution_subtract_fusion.6
  354.7 0.2 fusion.31
  355.0 16.8 %all-gather = f32[16,18,256]{2,1,0:T(8,128)S(1)} all-gather(f32[1,18,256]{2,1,0:T(8,128)S(1)} %fusion.49), channel_id=1, replica_groups=mesh['row'=32,'col'=16] {'col'}, dimensions={0}, use_global_device_ids=true | all-gather | bytes 313344 | tf_op jit(solution)/shard_map/all_gather | solution.py:45
  371.8 0.8 broadcast_select_fusion.2
  372.7 1.3 dynamic-slice.11
  374.7 154.2 %all-reduce.20.cloned.1.call-done = (f32[256,256]{0,1:T(8,128)}, f32[288,256]{1,0:T(8,128)}, f32[288,256]{1,0:T(8,128)}) async-done(((f32[256,256]{0,1:T(8,128)}, f32[288,256]{1,0:T(8,128)}, f32[288,256]{1,0:T(8,128)}), (f32[256,256]{0,1:T(8,128)}, f32[288,256]{1,0:T(8,128)}, f32[288,256]{1,0:T(8,128)})) %all-reduce.20.cloned.1.call-update) | async-done | bytes 851984 | tf_op jit(solution)/shard_map/psum | solution.py:40
  529.0 1.2 fusion.18
  530.2 1.3 convolution_subtract_fusion.3
  531.5 0.3 fusion.30
  531.8 0.4 fusion.11
  532.3 0.2 copy-done.3
  532.5 0.3 copy-done.2
  532.8 0.6 copy-done
  533.4 0.9 convolution_bitcast_fusion
  534.3 0.9 copy.11
  535.3 0.1 copy.13
  535.5 11.7 %cholesky.164 = f32[128,128]{1,0:T(8,128)S(1)} custom-call(f32[128,128]{1,0:T(8,128)S(1)} %cholesky.197), custom_call_target="Cholesky" | custom-call | tf_op jit(solution)/shard_map/jit(cholesky)/cholesky | solution.py:48
  547.3 9.8 custom-call.25
  557.1 0.2 constant_dynamic-update-slice_fusion.2
  557.3 0.3 convolution_subtract_fusion.4
  557.6 11.7 %cholesky.181 = f32[128,128]{1,0:T(8,128)S(1)} custom-call(f32[128,128]{1,0:T(8,128)S(1)} %convolution_subtract_fusion.4), custom_call_target="Cholesky" | custom-call | tf_op jit(solution)/shard_map/jit(cholesky)/cholesky | solution.py:48
  569.3 0.7 compare_reduce_fusion
  570.0 0.7 compare_reduce_fusion.1
  572.0 4.3 while.7
  572.2 0.6 fusion.77
  572.9 1.3 bitcast_dynamic-update-slice_fusion.5
  574.2 0.6 fusion.77
  574.9 1.3 bitcast_dynamic-update-slice_fusion.5
  576.2 19.7 %custom-call.20 = f32[2,128,128]{1,2,0:T(8,128)S(1)} custom-call(f32[2,128,128]{2,1,0:T(8,128)S(1)} %get-tuple-element.30), custom_call_target="InvertDiagBlocksLowerTriangular" | custom-call | tf_op jit(solution)/shard_map/jit(_cho_solve)/triangular_solve | solution.py:48
  595.9 0.3 fusion.16
  596.2 0.3 convolution_subtract_fusion.2
  596.5 0.3 fusion.33
  596.8 0.3 fusion.34
  597.1 0.3 convolution_subtract_fusion.1
  597.4 0.3 fusion.32
  597.7 49.2 %all-reduce.16.cloned.1.call-done = f32[288,256]{0,1:T(8,128)} async-done(((f32[288,256]{0,1:T(8,128)}), f32[288,256]{0,1:T(8,128)}) %all-reduce.16.cloned.1.call-update) | async-done | bytes 294928
  646.8 1.3 fusion.15
  648.2 1.2 fusion.47
  649.5 275.7 %all-reduce.14.cloned.1.call-done = f32[256,256]{1,0:T(8,128)} async-done(((f32[256,256]{1,0:T(8,128)}), f32[256,256]{1,0:T(8,128)}) %all-reduce.14.cloned.1.call-update) | async-done | bytes 262160 | tf_op jit(solution)/shard_map/psum | solution.py:53
  925.2 1.5 fusion.14
  926.7 0.3 fusion.6
  927.0 15.7 %all-gather.1 = f32[16,18,256]{2,1,0:T(8,128)S(1)} all-gather(f32[1,18,256]{2,1,0:T(8,128)S(1)} %fusion.6), channel_id=1, replica_groups=mesh['row'=32,'col'=16] {'col'}, dimensions={0}, use_global_device_ids=true | all-gather | bytes 313344 | tf_op jit(solution)/shard_map/all_gather | solution.py:56
  942.8 0.8 broadcast_select_fusion.1
  943.6 157.6 %all-reduce.18.cloned.1.call-done = (f32[288,256]{1,0:T(8,128)}, f32[288,256]{1,0:T(8,128)}) async-done(((f32[288,256]{1,0:T(8,128)}, f32[288,256]{1,0:T(8,128)}), (f32[288,256]{1,0:T(8,128)}, f32[288,256]{1,0:T(8,128)})) %all-reduce.18.cloned.1.call-update) | async-done | bytes 589840 | tf_op jit(solution)/shard_map/psum | solution.py:9
  1101.2 3.5 convolution_subtract_fusion
  (43 shorter events, 1.0 us)
Async XLA Ops:
  6.5 122.9 %all-reduce.22.cloned.1.call-start = ((), (), s32[]{:S(2)}) async-start(), calls=%async_computation.5 | async-start | bytes 1048576 | tf_op jit(solution)/shard_map/psum | solution.py:40
  10.2 282.2 %all-reduce.12.cloned.1.call-start = ((), (), s32[]{:S(2)}) async-start(), calls=%async_computation | async-start | bytes 524288 | tf_op jit(solution)/shard_map/psum | solution.py:40
  129.5 399.5 %all-reduce.20.cloned.1.call-start = ((), (), s32[]{:S(2)}) async-start(), calls=%async_computation.4 | async-start | bytes 1703936 | tf_op jit(solution)/shard_map/psum | solution.py:40
  330.3 24.1 %copy-start.1 = (f32[18,256]{1,0:T(8,128)S(1)}, f32[18,256]{1,0:T(8,128)}, u32[]{:S(2)}) copy-start(f32[18,256]{1,0:T(8,128)} %param.5) | copy-start | bytes 55300
  372.7 274.2 %all-reduce.16.cloned.1.call-start = ((), (), s32[]{:S(2)}) async-start(), calls=%async_computation.2 | async-start | bytes 786432
  531.5 1.0 copy-start.3
  531.8 1.0 copy-start.2
  532.2 1.2 copy-start
  535.3 389.9 %all-reduce.14.cloned.1.call-start = ((), (), s32[]{:S(2)}) async-start(), calls=%async_computation.1 | async-start | bytes 524288 | tf_op jit(solution)/shard_map/psum | solution.py:53
  649.4 451.8 %all-reduce.18.cloned.1.call-start = ((), (), s32[]{:S(2)}) async-start(), calls=%async_computation.3 | async-start | bytes 1179648 | tf_op jit(solution)/shard_map/psum | solution.py:9
Sparse Core Ops, SparseCore 0:
  10.3 119.1 all-reduce.21
  132.9 159.4 all-reduce.11
  372.8 156.1 all-reduce.19
  535.4 111.4 all-reduce.15
  651.7 273.4 all-reduce.13
  943.8 157.4 all-reduce.17
